TPU v7x, 512 devices: a whole 4x4x16 slice. The times are simulated.
512 devices in a mesh: segment: 2 (over core), lat: 64 (over x, z_lo, y), tok: 4 (over z_hi).
Axes of the slice: x: 4, y: 4, z: 16 (z_hi: 4, z_lo: 4; z = z_hi * 4 + z_lo), core: 2. Of those that a mesh axis runs over, the one named last changes fastest.
Arguments:
- resid_mid: bfloat16 [512, 4608], P('lat', ('segment', 'tok'))
- mlp_out: bfloat16 [512, 4608], P('lat', ('segment', 'tok'))
- post_gain: float32 [4608], P(('segment', 'tok')), may hold values from 0.5 to 1.5
- enc_weight: bfloat16 [4608, 65536], P(('segment', 'tok'), 'lat'), may hold values from -0.09375 to 0.09375
- enc_bias: float32 [65536], P('lat'), may hold values from -3 to 3
- dec_weight: bfloat16 [65536, 4608], P('lat', ('segment', 'tok')), may hold values from -0.046875 to 0.046875
- dec_bias: float32 [4608], P(('segment', 'tok')), may hold values from -3 to 3
- panel_lists: int32 [4, 128], replicated, may hold values from 0 to 511, as said below
Outputs:
- sq_error: float32 [], replicated
- enc_grad: bfloat16 [4608, 65536], P(('segment', 'tok'), 'lat')
- dec_grad: bfloat16 [65536, 4608], P('lat', ('segment', 'tok'))
Inputs may be any that keep to these rules, and one draw needn't show every extreme that they name: `panel_lists`: each row lists 128 different panels.
All inputs are finite; a program needn't handle non-finite values.
Results may differ from a plain program's by a relative error of at most 0.014.
Values may be sent and summed in bfloat16 or wider, within the bound.
A program may use at most 64 MiB of HBM per device.

v0:
```python
import jax
import jax.numpy as jnp
from jax import lax
from jax.sharding import PartitionSpec as P

D = 4608
PANEL = 128
BLOCK = 128


def gelu_pair(preact):
    activation, pullback = jax.vjp(jax.nn.gelu, preact)
    return (activation, pullback(jnp.ones_like(preact))[0])


def on_device(
    resid_mid, mlp_out, post_gain, enc_weight, enc_bias, dec_weight, dec_bias, panel_lists
):
    model_rows = mlp_out.astype(jnp.float32)
    squares_part = jnp.sum(model_rows * model_rows, axis=1)
    squares_total = lax.psum(squares_part, ("segment", "tok"))
    scale_rows = lax.rsqrt(squares_total / D + 1e-06)
    normed = model_rows * scale_rows[:, None] * post_gain[None, :]
    own_rows = (resid_mid.astype(jnp.float32) + normed).astype(jnp.bfloat16)
    features = lax.all_gather(own_rows, "lat", axis=0, tiled=True)
    token_count = features.shape[0]
    centered = (features.astype(jnp.float32) - dec_bias[None, :]).astype(jnp.bfloat16)
    encode_part = jnp.dot(centered, enc_weight, preferred_element_type=jnp.float32)
    preact = (
        lax.psum(encode_part.astype(jnp.bfloat16), ("segment", "tok")).astype(jnp.float32)
        + enc_bias[None, :]
    )
    panel_count = enc_weight.shape[1] // PANEL
    block_count = token_count // BLOCK
    panel_ids = lax.axis_index("lat") * panel_count + jnp.arange(panel_count, dtype=jnp.int32)
    active_flags = jnp.any(panel_lists[:, :, None] == panel_ids[None, None, :], axis=1).astype(
        jnp.float32
    )
    tile_mask = jnp.broadcast_to(
        active_flags[:, None, :, None], (block_count, BLOCK, panel_count, PANEL)
    ).reshape(token_count, enc_weight.shape[1])
    activation, derivative = gelu_pair(preact)
    latents = (activation * tile_mask).astype(jnp.bfloat16)
    decode_part = jnp.dot(latents, dec_weight, preferred_element_type=jnp.float32)
    rebuilt = lax.psum(decode_part, "lat") + dec_bias[None, :]
    error_full = rebuilt - features.astype(jnp.float32)
    error_sum = lax.psum(jnp.sum(error_full * error_full), ("segment", "tok"))
    error_bf = error_full.astype(jnp.bfloat16)
    sq_error = error_sum / (token_count * D)
    dec_grad = jnp.einsum(
        "tl,td->ld", latents, error_bf, preferred_element_type=jnp.float32
    ).astype(jnp.bfloat16)
    latent_part = jnp.einsum("td,ld->tl", error_bf, dec_weight, preferred_element_type=jnp.float32)
    latent_grad = lax.psum(latent_part.astype(jnp.bfloat16), ("segment", "tok")).astype(jnp.float32)
    pre_grad = (latent_grad * derivative * tile_mask).astype(jnp.bfloat16)
    enc_grad = jnp.einsum(
        "td,tl->dl", centered, pre_grad, preferred_element_type=jnp.float32
    ).astype(jnp.bfloat16)
    return (sq_error, enc_grad, dec_grad)


def solution(mesh):
    placed = (
        P("lat", ("segment", "tok")),
        P("lat", ("segment", "tok")),
        P(("segment", "tok")),
        P(("segment", "tok"), "lat"),
        P("lat"),
        P("lat", ("segment", "tok")),
        P(("segment", "tok")),
        P(),
    )
    return jax.shard_map(
        on_device,
        mesh=mesh,
        in_specs=placed,
        out_specs=(P(), P(("segment", "tok"), "lat"), P("lat", ("segment", "tok"))),
        check_vma=False,
    )
```

profile of v0, /device:TPU:15, one launch (start us, length us, event | category | flops | bytes accessed | tf_op | source)
XLA Modules:
  0.0 1230.6 jit_solution(12697475132606442277)
XLA Ops:
  7.2 0.0 copy-start
  7.2 0.0 all-reduce.4.cloned.1.call-start
  7.2 0.9 fusion.17
  8.1 30.3 %psum.35 = f32[8]{0:T(128)S(1)} all-reduce(f32[8]{0:T(128)S(1)} %fusion.17), channel_id=1, replica_groups=mesh['segment'=2,'lat'=64,'tok'=4] {'segment','tok'}, use_global_device_ids=true, to_apply=%region_1.0 | all-reduce | flops 8 | bytes 64 | tf_op jit(solution)/shard_map/psum | solution.py:21
  38.5 0.8 fusion.20
  39.3 135.7 %all_gather.3 = bf16[512,576]{1,0:T(8,128)(2,1)S(1)} all-gather(bf16[8,576]{1,0:T(8,128)(2,1)S(1)} %fusion.20), channel_id=1, replica_groups=mesh['segment'=2,'lat'=64,'tok'=4] {'lat'}, dimensions={0}, use_global_device_ids=true | all-gather | bytes 599040 | tf_op jit(solution)/shard_map/all_gather | solution.py:25
  175.0 0.2 copy.16
  175.2 0.0 copy-start.1
  175.3 0.0 copy-start.7
  175.3 3.6 convolution_convert_fusion.3
  178.8 0.0 copy-done.1
  178.8 0.0 copy-start.5
  178.8 0.0 all-reduce.4.cloned.1.call-update
  178.9 0.0 all-reduce.6.cloned.1.call-start
  178.9 0.0 copy-done.7
  178.9 0.2 compare_reduce_fusion
  179.2 190.6 %all-reduce.4.cloned.1.call-done = bf16[512,1024]{1,0:T(8,128)(2,1)} async-done(((bf16[512,1024]{1,0:T(8,128)(2,1)}), bf16[512,1024]{1,0:T(8,128)(2,1)}) %all-reduce.4.cloned.1.call-update) | async-done | bytes 1048592 | tf_op jit(solution)/shard_map/psum | solution.py:30
  369.8 0.0 copy-start.2
  369.8 0.2 broadcast_in_dim.2
  370.0 0.0 copy-done.5
  370.0 1.0 copy-done.2
  371.0 1.0 fusion.9
  371.9 0.0 copy-start.3
  372.0 1.0 copy-done.3
  372.9 0.0 copy-done
  372.9 0.0 copy-start.6
  372.9 1.8 fusion.27
  374.8 0.0 all-reduce.6.cloned.1.call-update
  374.8 0.0 all-reduce.8.cloned.1.call-start
  374.8 630.7 %all-reduce.6.cloned.1.call-done = f32[512,576]{0,1:T(8,128)} async-done(((f32[512,576]{0,1:T(8,128)}), f32[512,576]{0,1:T(8,128)}) %all-reduce.6.cloned.1.call-update) | async-done | bytes 1179664 | tf_op jit(solution)/shard_map/psum | solution.py:45
  1005.6 0.0 copy-done.6
  1005.6 2.5 fusion.14
  1008.1 0.0 copy-start.4
  1008.1 0.8 copy-done.4
  1008.9 2.0 convolution_convert_fusion.2
  1010.9 0.0 all-reduce.8.cloned.1.call-update
  1010.9 66.1 %psum.38 = f32[]{:T(128)} all-reduce(f32[]{:T(128)} %get-tuple-element.4), channel_id=1, replica_groups=mesh['segment'=2,'lat'=64,'tok'=4] {'segment','tok'}, use_global_device_ids=true, to_apply=%region_6.0 | all-reduce | flops 1 | bytes 8 | tf_op jit(solution)/shard_map/psum | solution.py:47
  1077.6 3.2 convolution_convert_fusion
  1080.8 137.0 %all-reduce.8.cloned.1.call-done = bf16[512,1024]{1,0:T(8,128)(2,1)} async-done(((bf16[512,1024]{1,0:T(8,128)(2,1)}), bf16[512,1024]{1,0:T(8,128)(2,1)}) %all-reduce.8.cloned.1.call-update) | async-done | bytes 1048592 | tf_op jit(solution)/shard_map/psum | solution.py:54
  1217.8 5.1 convolution_convert_fusion.1
  (3 shorter events, 0.0 us)
Async XLA Ops:
  7.2 365.8 %copy-start = (bf16[1024,576]{0,1:T(8,128)(2,1)S(1)}, bf16[1024,576]{0,1:T(8,128)(2,1)}, u32[]{:S(2)}) copy-start(bf16[1024,576]{0,1:T(8,128)(2,1)} %param.13) | copy-start | bytes 3538948
  7.2 362.6 %all-reduce.4.cloned.1.call-start = ((), (), s32[]{:S(2)}) async-start(), calls=%async_computation | async-start | bytes 2097152 | tf_op jit(solution)/shard_map/psum | solution.py:30
  175.2 3.6 copy-start.1
  175.3 3.7 copy-start.7
  178.8 191.1 %copy-start.5 = (f32[1024]{0:T(1024)S(1)}, f32[1024]{0:T(1024)}, u32[]{:S(2)}) copy-start(f32[1024]{0:T(1024)} %param.12) | copy-start | bytes 12292
  178.9 826.7 %all-reduce.6.cloned.1.call-start = ((), (), s32[]{:S(2)}) async-start(), calls=%async_computation.1 | async-start | bytes 2359296 | tf_op jit(solution)/shard_map/psum | solution.py:45
  369.8 1.2 copy-start.2
  371.9 1.0 copy-start.3
  372.9 632.7 %copy-start.6 = (f32[576]{0:T(1024)S(1)}, f32[576]{0:T(1024)}, u32[]{:S(2)}) copy-start(f32[576]{0:T(1024)} %param.14) | copy-start | bytes 6916
  374.8 843.0 %all-reduce.8.cloned.1.call-start = ((), (), s32[]{:S(2)}) async-start(), calls=%async_computation.2 | async-start | bytes 2097152 | tf_op jit(solution)/shard_map/psum | solution.py:54
  1008.1 0.8 copy-start.4
Sparse Core Ops, SparseCore 0:
  179.0 190.7 all-reduce.3
  374.9 630.6 all-reduce.5
  1011.0 206.7 all-reduce.7
where the time goes:
time: 1230 us
  waiting for transfers between devices  958 us (78%)
  blocking collectives  232 us (19%)
  matrix products  15.7 us (1%)
  between operations  15.6 us (1%)
    psum x1, waiting for transfers between devices, on_device(): rebuilt = lax.psum(decode_part, 'lat') + dec_bias[None, :]  631 us
    psum x1, waiting for transfers between devices, on_device(): lax.psum(encode_part.astype(jnp.bfloat16), ('segment', 'tok'))  191 us
    psum x1, waiting for transfers between devices, on_device(): lax.psum(latent_part.astype(jnp.bfloat16), ('segment', 'tok'))  137 us
    all_gather x1, blocking collectives, on_device(): features = lax.all_gather(own_rows, 'lat', axis=0, tiled=True)  136 us
    psum x1, blocking collectives, on_device(): error_sum = lax.psum(jnp.sum(error_full * error_full), ('segment', 'tok'))  66.1 us
    psum x1, blocking collectives, on_device(): squares_total = lax.psum(squares_part, ('segment', 'tok'))  30.3 us
  transfers between devices with their start and end apart: 3, of which 3 were waited for; matrix products, arithmetic and copies ran while one was open for 0% of the time, Pallas kernels for 0%

commit v1 on v0

--- a/solution.py
+++ b/solution.py
@@ -22,7 +22,9 @@
     scale_rows = lax.rsqrt(squares_total / D + 1e-06)
     normed = model_rows * scale_rows[:, None] * post_gain[None, :]
     own_rows = (resid_mid.astype(jnp.float32) + normed).astype(jnp.bfloat16)
-    features = lax.all_gather(own_rows, "lat", axis=0, tiled=True)
+    features = jnp.concatenate(
+        lax.all_to_all(jnp.stack([own_rows] * lax.axis_size("lat")), "lat", 0, 0), axis=0
+    )
     token_count = features.shape[0]
     centered = (features.astype(jnp.float32) - dec_bias[None, :]).astype(jnp.bfloat16)
     encode_part = jnp.dot(centered, enc_weight, preferred_element_type=jnp.float32)

time: 1230 us -> 1080 us (0.88)
  blocking collectives: 232 us -> 122 us
  waiting for transfers between devices: 958 us -> 911 us
    all_gather x1 -> x0, blocking collectives: 136 us -> none  [on_device(): features = lax.all_gather(own_rows, 'lat', axis=0, tiled=True)]
    psum x1, waiting for transfers between devices: 191 us -> 143 us  [on_device(): lax.psum(encode_part.astype(jnp.bfloat16), ('segment', 'tok'))]
    all_to_all x0 -> x1, blocking collectives: none -> 26.1 us  [on_device(): lax.all_to_all(jnp.stack([own_rows] * lax.axis_size('lat')), 'lat', 0, 0)]
where the time goes in v1:
time: 1080 us; the launch traced here: 1070 us
  waiting for transfers between devices  911 us (84%)
  blocking collectives  122 us (11%)
  matrix products  16 us (1%)
  between operations  15.6 us (1%)
    psum x1, waiting for transfers between devices, on_device(): rebuilt = lax.psum(decode_part, 'lat') + dec_bias[None, :]  630 us
    psum x1, waiting for transfers between devices, on_device(): lax.psum(encode_part.astype(jnp.bfloat16), ('segment', 'tok'))  143 us
    psum x1, waiting for transfers between devices, on_device(): lax.psum(latent_part.astype(jnp.bfloat16), ('segment', 'tok'))  138 us
    psum x1, blocking collectives, on_device(): error_sum = lax.psum(jnp.sum(error_full * error_full), ('segment', 'tok'))  66.1 us
    psum x1, blocking collectives, on_device(): squares_total = lax.psum(squares_part, ('segment', 'tok'))  30.3 us
    all_to_all x1, blocking collectives, on_device(): lax.all_to_all(jnp.stack([own_rows] * lax.axis_size('lat')), 'lat', 0, 0)  26.1 us
  transfers between devices with their start and end apart: 3, of which 3 were waited for; matrix products, arithmetic and copies ran while one was open for 0% of the time, Pallas kernels for 0%

profile of v1, /device:TPU:15, one launch (start us, length us, event | category | flops | bytes accessed | tf_op | source)
XLA Modules:
  0.0 1075.0 jit_solution(1193891837666823515)
XLA Ops:
  7.2 0.0 copy-start
  7.2 0.0 all-reduce.4.cloned.1.call-start
  7.2 0.9 fusion.15
  8.1 30.3 %psum.35 = f32[8]{0:T(128)S(1)} all-reduce(f32[8]{0:T(128)S(1)} %fusion.15), channel_id=1, replica_groups=mesh['segment'=2,'lat'=64,'tok'=4] {'segment','tok'}, use_global_device_ids=true, to_apply=%region_1.0 | all-reduce | flops 8 | bytes 64 | tf_op jit(solution)/shard_map/psum | solution.py:21
  38.5 0.8 fusion.18
  39.3 0.1 stack.2
  39.3 26.1 %all_to_all.5 = bf16[64,8,576]{2,1,0:T(8,128)(2,1)S(1)} all-to-all(bf16[64,8,576]{2,1,0:T(8,128)(2,1)S(1)} %stack.2), channel_id=1, replica_groups=mesh['segment'=2,'lat'=64,'tok'=4] {'lat'}, dimensions={0} | all-to-all | bytes 1179648 | tf_op jit(solution)/shard_map/all_to_all | solution.py:26
  65.4 0.0 copy-start.4
  65.4 0.1 bitcast_convert_fusion
  65.5 1.4 copy.14
  66.9 0.0 copy-done.4
  66.9 0.0 copy-start.6
  66.9 3.7 convolution_convert_fusion.3
  70.6 0.0 copy-start.5
  70.6 0.0 all-reduce.4.cloned.1.call-update
  70.6 0.0 all-reduce.6.cloned.1.call-start
  70.7 0.0 copy-done.6
  70.7 0.2 compare_reduce_fusion
  70.9 142.7 %all-reduce.4.cloned.1.call-done = bf16[512,1024]{1,0:T(8,128)(2,1)} async-done(((bf16[512,1024]{1,0:T(8,128)(2,1)}), bf16[512,1024]{1,0:T(8,128)(2,1)}) %all-reduce.4.cloned.1.call-update) | async-done | bytes 1048592 | tf_op jit(solution)/shard_map/psum | solution.py:32
  213.7 0.0 copy-start.1
  213.7 0.2 broadcast_in_dim.2
  213.9 0.0 copy-done.5
  213.9 1.0 copy-done.1
  214.9 1.0 fusion.9
  215.9 0.0 copy-start.2
  215.9 1.0 copy-done.2
  216.9 0.0 copy-done
  216.9 1.8 fusion.25
  218.7 0.0 all-reduce.6.cloned.1.call-update
  218.7 0.0 all-reduce.8.cloned.1.call-start
  218.8 630.0 %all-reduce.6.cloned.1.call-done = f32[512,576]{0,1:T(8,128)} async-done(((f32[512,576]{0,1:T(8,128)}), f32[512,576]{0,1:T(8,128)}) %all-reduce.6.cloned.1.call-update) | async-done | bytes 1179664 | tf_op jit(solution)/shard_map/psum | solution.py:47
  848.8 2.7 multiply_reduce_fusion
  851.4 0.0 copy-start.3
  851.4 0.8 copy-done.3
  852.2 2.0 convolution_convert_fusion.2
  854.2 0.0 all-reduce.8.cloned.1.call-update
  854.3 66.1 %psum.38 = f32[]{:T(128)} all-reduce(f32[]{:T(128)} %get-tuple-element.3), channel_id=1, replica_groups=mesh['segment'=2,'lat'=64,'tok'=4] {'segment','tok'}, use_global_device_ids=true, to_apply=%region_6.0 | all-reduce | flops 1 | bytes 8 | tf_op jit(solution)/shard_map/psum | solution.py:49
  921.0 3.2 convolution_convert_fusion
  924.2 137.8 %all-reduce.8.cloned.1.call-done = bf16[512,1024]{1,0:T(8,128)(2,1)} async-done(((bf16[512,1024]{1,0:T(8,128)(2,1)}), bf16[512,1024]{1,0:T(8,128)(2,1)}) %all-reduce.8.cloned.1.call-update) | async-done | bytes 1048592 | tf_op jit(solution)/shard_map/psum | solution.py:56
  1062.0 5.3 convolution_convert_fusion.1
  (3 shorter events, 0.0 us)
Async XLA Ops:
  7.2 209.7 %copy-start = (bf16[1024,576]{0,1:T(8,128)(2,1)S(1)}, bf16[1024,576]{0,1:T(8,128)(2,1)}, u32[]{:S(2)}) copy-start(bf16[1024,576]{0,1:T(8,128)(2,1)} %param.13) | copy-start | bytes 3538948
  7.2 206.5 %all-reduce.4.cloned.1.call-start = ((), (), s32[]{:S(2)}) async-start(), calls=%async_computation.1 | async-start | bytes 2097152 | tf_op jit(solution)/shard_map/psum | solution.py:32
  65.4 1.5 copy-start.4
  66.9 3.8 copy-start.6
  70.6 143.3 %copy-start.5 = (f32[1024]{0:T(1024)S(1)}, f32[1024]{0:T(1024)}, u32[]{:S(2)}) copy-start(f32[1024]{0:T(1024)} %param.12) | copy-start | bytes 12292
  70.6 778.1 %all-reduce.6.cloned.1.call-start = ((), (), s32[]{:S(2)}) async-start(), calls=%async_computation.2 | async-start | bytes 2359296 | tf_op jit(solution)/shard_map/psum | solution.py:47
  213.7 1.2 copy-start.1
  215.9 1.0 copy-start.2
  218.7 843.3 %all-reduce.8.cloned.1.call-start = ((), (), s32[]{:S(2)}) async-start(), calls=%async_computation.3 | async-start | bytes 2097152 | tf_op jit(solution)/shard_map/psum | solution.py:56
  851.4 0.8 copy-start.3
Sparse Core Ops, SparseCore 0:
  70.8 142.8 all-reduce.3
  218.8 629.8 all-reduce.5
  854.4 207.6 all-reduce.7

commit v2 on v0

--- a/solution.py
+++ b/solution.py
@@ -18,7 +18,7 @@
 ):
     model_rows = mlp_out.astype(jnp.float32)
     squares_part = jnp.sum(model_rows * model_rows, axis=1)
-    squares_total = lax.psum(squares_part, ("segment", "tok"))
+    squares_total = jnp.sum(lax.all_gather(squares_part, ("segment", "tok")), axis=0)
     scale_rows = lax.rsqrt(squares_total / D + 1e-06)
     normed = model_rows * scale_rows[:, None] * post_gain[None, :]
     own_rows = (resid_mid.astype(jnp.float32) + normed).astype(jnp.bfloat16)

time: 1230 us -> 1230 us (level)
    psum x1 -> x0, blocking collectives: 30.3 us -> none  [on_device(): squares_total = lax.psum(squares_part, ('segment', 'tok'))]
    unnamed x0 -> x1, blocking collectives: none -> 30.3 us
where the time goes in v2:
time: 1230 us
  waiting for transfers between devices  960 us (78%)
  blocking collectives  232 us (19%)
  between operations  16.3 us (1%)
  matrix products  15.7 us (1%)
    psum x1, waiting for transfers between devices, on_device(): rebuilt = lax.psum(decode_part, 'lat') + dec_bias[None, :]  630 us
    psum x1, waiting for transfers between devices, on_device(): lax.psum(encode_part.astype(jnp.bfloat16), ('segment', 'tok'))  193 us
    psum x1, waiting for transfers between devices, on_device(): lax.psum(latent_part.astype(jnp.bfloat16), ('segment', 'tok'))  137 us
    all_gather x1, blocking collectives, on_device(): features = lax.all_gather(own_rows, 'lat', axis=0, tiled=True)  136 us
    psum x1, blocking collectives, on_device(): error_sum = lax.psum(jnp.sum(error_full * error_full), ('segment', 'tok'))  66.1 us
    unnamed x1, blocking collectives  30.3 us
  transfers between devices with their start and end apart: 3, of which 3 were waited for; matrix products, arithmetic and copies ran while one was open for 0% of the time, Pallas kernels for 0%

profile of v2, /device:TPU:15, one launch (start us, length us, event | category | flops | bytes accessed | tf_op | source)
XLA Modules:
  0.0 1234.4 jit_solution(14720920746668320095)
XLA Ops:
  7.2 0.0 copy-start
  7.2 0.0 all-reduce.5.cloned.1.call-start
  7.2 0.9 fusion.17
  8.1 1.3 dynamic-slice
  10.1 0.2 dynamic-update-slice
  10.3 30.3 %all-reduce = f32[64]{0:T(128)S(1)} all-reduce(f32[64]{0:T(128)S(1)} %dynamic-update-slice), channel_id=2, replica_groups=mesh['segment'=2,'lat'=64,'tok'=4] {'segment','tok'}, use_global_device_ids=true, to_apply=%add | all-reduce | flops 64 | bytes 512
  40.6 0.1 reshape.26
  40.8 0.8 fusion.20
  41.6 135.7 %all_gather.11 = bf16[512,576]{1,0:T(8,128)(2,1)S(1)} all-gather(bf16[8,576]{1,0:T(8,128)(2,1)S(1)} %fusion.20), channel_id=1, replica_groups=mesh['segment'=2,'lat'=64,'tok'=4] {'lat'}, dimensions={0}, use_global_device_ids=true | all-gather | bytes 599040 | tf_op jit(solution)/shard_map/all_gather | solution.py:25
  177.3 0.2 copy.16
  177.5 0.0 copy-start.1
  177.5 0.0 copy-start.7
  177.5 3.6 convolution_convert_fusion.3
  181.1 0.0 copy-done.1
  181.1 0.0 copy-start.5
  181.1 0.0 all-reduce.5.cloned.1.call-update
  181.1 0.0 all-reduce.7.cloned.1.call-start
  181.2 0.0 copy-done.7
  181.2 0.2 compare_reduce_fusion
  181.4 192.5 %all-reduce.5.cloned.1.call-done = bf16[512,1024]{1,0:T(8,128)(2,1)} async-done(((bf16[512,1024]{1,0:T(8,128)(2,1)}), bf16[512,1024]{1,0:T(8,128)(2,1)}) %all-reduce.5.cloned.1.call-update) | async-done | bytes 1048592 | tf_op jit(solution)/shard_map/psum | solution.py:30
  374.0 0.0 copy-start.2
  374.0 0.2 broadcast_in_dim.2
  374.2 0.0 copy-done.5
  374.2 1.0 copy-done.2
  375.2 1.0 fusion.9
  376.1 0.0 copy-start.3
  376.2 1.0 copy-done.3
  377.1 0.0 copy-done
  377.1 0.0 copy-start.6
  377.1 1.8 fusion.27
  379.0 0.0 all-reduce.7.cloned.1.call-update
  379.0 0.0 all-reduce.9.cloned.1.call-start
  379.0 630.0 %all-reduce.7.cloned.1.call-done = f32[512,576]{0,1:T(8,128)} async-done(((f32[512,576]{0,1:T(8,128)}), f32[512,576]{0,1:T(8,128)}) %all-reduce.7.cloned.1.call-update) | async-done | bytes 1179664 | tf_op jit(solution)/shard_map/psum | solution.py:45
  1009.1 0.0 copy-done.6
  1009.1 2.5 fusion.14
  1011.6 0.0 copy-start.4
  1011.6 0.8 copy-done.4
  1012.4 2.0 convolution_convert_fusion.2
  1014.4 0.0 all-reduce.9.cloned.1.call-update
  1014.4 66.1 %psum.30 = f32[]{:T(128)} all-reduce(f32[]{:T(128)} %get-tuple-element.4), channel_id=1, replica_groups=mesh['segment'=2,'lat'=64,'tok'=4] {'segment','tok'}, use_global_device_ids=true, to_apply=%region_6.0 | all-reduce | flops 1 | bytes 8 | tf_op jit(solution)/shard_map/psum | solution.py:47
  1081.1 3.2 convolution_convert_fusion
  1084.3 137.3 %all-reduce.9.cloned.1.call-done = bf16[512,1024]{1,0:T(8,128)(2,1)} async-done(((bf16[512,1024]{1,0:T(8,128)(2,1)}), bf16[512,1024]{1,0:T(8,128)(2,1)}) %all-reduce.9.cloned.1.call-update) | async-done | bytes 1048592 | tf_op jit(solution)/shard_map/psum | solution.py:54
  1221.7 5.1 convolution_convert_fusion.1
  (5 shorter events, 0.0 us)
Async XLA Ops:
  7.2 370.0 %copy-start = (bf16[1024,576]{0,1:T(8,128)(2,1)S(1)}, bf16[1024,576]{0,1:T(8,128)(2,1)}, u32[]{:S(2)}) copy-start(bf16[1024,576]{0,1:T(8,128)(2,1)} %param.13) | copy-start | bytes 3538948
  7.2 366.8 %all-reduce.5.cloned.1.call-start = ((), (), s32[]{:S(2)}) async-start(), calls=%async_computation | async-start | bytes 2097152 | tf_op jit(solution)/shard_map/psum | solution.py:30
  177.5 3.6 copy-start.1
  177.5 3.7 copy-start.7
  181.1 193.1 %copy-start.5 = (f32[1024]{0:T(1024)S(1)}, f32[1024]{0:T(1024)}, u32[]{:S(2)}) copy-start(f32[1024]{0:T(1024)} %param.12) | copy-start | bytes 12292
  181.1 827.9 %all-reduce.7.cloned.1.call-start = ((), (), s32[]{:S(2)}) async-start(), calls=%async_computation.1 | async-start | bytes 2359296 | tf_op jit(solution)/shard_map/psum | solution.py:45
  374.0 1.2 copy-start.2
  376.1 1.0 copy-start.3
  377.1 631.9 %copy-start.6 = (f32[576]{0:T(1024)S(1)}, f32[576]{0:T(1024)}, u32[]{:S(2)}) copy-start(f32[576]{0:T(1024)} %param.14) | copy-start | bytes 6916
  379.0 842.7 %all-reduce.9.cloned.1.call-start = ((), (), s32[]{:S(2)}) async-start(), calls=%async_computation.2 | async-start | bytes 2097152 | tf_op jit(solution)/shard_map/psum | solution.py:54
  1011.6 0.8 copy-start.4
Sparse Core Ops, SparseCore 0:
  181.3 192.6 all-reduce.4
  379.1 629.8 all-reduce.6
  1014.5 207.1 all-reduce.8
